TPU v7x, 32 devices: a whole 2x2x4 slice. The times are simulated.
32 devices in a mesh: grp: 2 (over x), px: 4 (over y, core), py: 4 (over z).
Axes of the slice: x: 2, y: 2, z: 4, core: 2. Of those that a mesh axis runs over, the one named last changes fastest.
Arguments:
- multiplier: float32 [3, 32, 16, 256, 256], P(None, 'py', None, ('grp', 'px')), may hold values from -6 to 6
- auxiliary: float32 [3, 32, 16, 256, 256], P(None, 'py', None, ('grp', 'px')), may hold values from -6 to 6
- density_start: float32 [16, 256, 256], P(None, ('grp', 'px')), may hold values from 0.5 to 2
- density_end: float32 [16, 256, 256], P(None, ('grp', 'px')), may hold values from 0.5 to 2
Outputs:
- multiplier_next: float32 [3, 32, 16, 256, 256], P(None, 'py', None, ('grp', 'px'))
- auxiliary_next: float32 [3, 32, 16, 256, 256], P(None, 'py', None, ('grp', 'px'))
All inputs are finite; a program needn't handle non-finite values.
Results may differ from a plain program's by a relative error of at most 0.0003.
Values sent between devices are 32-bit elements; how exact they have to be, the bound alone decides.
A program may use at most 128 MiB of HBM per device.

v0:
```python
import math

import jax
import jax.numpy as jnp
from jax import lax
from jax.sharding import PartitionSpec as P

NEWTON = 4


PENALTY = 1.0
PRECISE = lax.Precision.HIGHEST


def passed_along(value, axis, steps):
    count = lax.axis_size(axis)
    initial, last = (max(0, -steps), min(count, count - steps))
    return lax.ppermute(value, axis, [(source, source + steps) for source in range(initial, last)])


def from_behind(block, axis, distance):
    devices = range(lax.axis_size(axis))
    route = [((i - distance) % len(devices), i) for i in devices]
    return lax.ppermute(block, axis, route)


def cosine_table(levels):
    mode_index = lax.broadcasted_iota(jnp.int32, (levels, levels), 0)
    time_index = lax.broadcasted_iota(jnp.int32, (levels, levels), 1)
    phase_index = mode_index * (2 * time_index + 1) % (4 * levels)
    angles = phase_index.astype(jnp.float32) * (math.pi / (2 * levels))
    weights = jnp.where(mode_index == 0, math.sqrt(1.0 / levels), math.sqrt(2.0 / levels))
    return weights * jnp.cos(angles)


def difference_table(cosine):
    levels = cosine.shape[0]
    later = jnp.concatenate([cosine[:, 1:], jnp.zeros_like(cosine[:, :1])], axis=1)
    time_index = lax.broadcasted_iota(jnp.int32, (levels, levels), 1)
    return jnp.where(time_index < levels - 1, later - cosine, 0.0)


def hartley_table(length):
    row_index = lax.broadcasted_iota(jnp.int32, (length, length), 0)
    col_index = lax.broadcasted_iota(jnp.int32, (length, length), 1)
    phase_index = row_index * col_index % length
    angles = phase_index.astype(jnp.float32) * (2.0 * math.pi / length)
    return (jnp.cos(angles) + jnp.sin(angles)) / math.sqrt(length)


def spatial(field, hartley_rows, hartley_cols):
    field = jnp.einsum("ctbxy,kx->ctbky", field, hartley_rows, precision=PRECISE)
    return jnp.einsum("ctbxy,ky->ctbxk", field, hartley_cols, precision=PRECISE)


def eigenvalues(levels, row_start, row_total, row_count, col_count):
    time_modes = lax.broadcasted_iota(jnp.int32, (levels, 1, 1, 1), 0).astype(jnp.float32)
    row_modes = (row_start + lax.broadcasted_iota(jnp.int32, (1, 1, row_total, 1), 2)).astype(
        jnp.float32
    )
    col_modes = lax.broadcasted_iota(jnp.int32, (1, 1, 1, col_count), 3).astype(jnp.float32)
    time_part = 4.0 * jnp.sin(time_modes * (math.pi / (2 * levels))) ** 2
    row_part = 4.0 * jnp.sin(row_modes * (math.pi / row_count)) ** 2
    col_part = 4.0 * jnp.sin(col_modes * (math.pi / col_count)) ** 2
    return time_part + row_part + col_part


def project(target):
    time_part = target[0]
    space_first = target[1]
    space_second = target[2]
    kinetic = 0.5 * (space_first * space_first + space_second * space_second)
    offset_one = 1.0 + time_part
    scaling = jnp.maximum(offset_one, 1.0) + jnp.cbrt(kinetic)
    for newton_step in range(NEWTON):
        residue = scaling * scaling * (scaling - offset_one) - kinetic
        derivative = scaling * (3.0 * scaling - 2.0 * offset_one)
        scaling = jnp.maximum(scaling - residue / derivative, 1.0)
    feasible = time_part + kinetic <= 0.0
    return jnp.stack(
        [
            jnp.where(feasible, time_part, time_part - (scaling - 1.0)),
            jnp.where(feasible, space_first, space_first / scaling),
            jnp.where(feasible, space_second, space_second / scaling),
        ]
    )


def local(multiplier, auxiliary, density_start, density_end):
    levels_here = multiplier.shape[1]
    levels = levels_here * lax.axis_size("py")
    first_level = lax.axis_index("py") * levels_here
    level_index = first_level + lax.broadcasted_iota(jnp.int32, (levels_here, 1, 1, 1), 0)
    offset_field = auxiliary - multiplier / PENALTY
    offset_time = jnp.where(level_index == levels - 1, 0.0, offset_field[0])
    boundary = jnp.where(level_index == 0, -density_start / PENALTY, 0.0) + jnp.where(
        level_index == levels - 1, density_end / PENALTY, 0.0
    )
    offset_second = offset_field[2]
    source = jnp.roll(offset_second, 1, axis=3) - offset_second + boundary
    before = passed_along(offset_time[levels_here - 1 :], "py", 1)
    earlier = jnp.concatenate([before, offset_time[: levels_here - 1]], axis=0)
    offset_along = offset_field[1]
    rows_here = offset_along.shape[2]
    left_rim = from_behind(offset_along[:, :, rows_here - 1 :, :], ("grp", "px"), 1)
    beside = jnp.concatenate([left_rim, offset_along[:, :, : rows_here - 1, :]], axis=2)
    payload = (earlier - offset_time + beside - offset_along + source)[None]
    pencil = lax.all_to_all(payload, ("grp", "px"), split_axis=2, concat_axis=3, tiled=True)
    row_count = pencil.shape[3]
    col_count = pencil.shape[4]
    hartley_rows = hartley_table(row_count)
    hartley_cols = hartley_table(col_count)
    spectral = spatial(pencil, hartley_rows, hartley_cols)
    mode_data = lax.all_to_all(spectral, "py", split_axis=3, concat_axis=1, tiled=True)
    cosine = cosine_table(levels)
    difference = difference_table(cosine)
    rhs_modes = jnp.einsum("kt,tbxy->kbxy", cosine, mode_data[0], precision=PRECISE)
    rows_mode = mode_data.shape[3]
    eigen = eigenvalues(levels, lax.axis_index("py") * rows_mode, rows_mode, row_count, col_count)
    positive = eigen > 0.0
    inverse = jnp.where(positive, 1.0 / jnp.where(positive, eigen, 1.0), 0.0)
    potential_modes = rhs_modes * inverse
    potential = jnp.einsum("kt,kbxy->tbxy", cosine, potential_modes, precision=PRECISE)
    time_rate = jnp.einsum("kt,kbxy->tbxy", difference, potential_modes, precision=PRECISE)
    returned = lax.all_to_all(
        jnp.stack([potential, time_rate]), "py", split_axis=1, concat_axis=3, tiled=True
    )
    space_values = spatial(returned, hartley_rows, hartley_cols)
    plane_potential = space_values[0]
    gradient = jnp.stack(
        [
            space_values[1],
            jnp.roll(plane_potential, -1, axis=2) - plane_potential,
            jnp.roll(plane_potential, -1, axis=3) - plane_potential,
        ]
    )
    slab_gradient = lax.all_to_all(gradient, ("grp", "px"), split_axis=3, concat_axis=2, tiled=True)
    target = slab_gradient + multiplier / PENALTY
    auxiliary_next = project(target)
    multiplier_next = multiplier + PENALTY * (slab_gradient - auxiliary_next)
    return (multiplier_next, auxiliary_next)


def solution(mesh):
    placed = (
        P(None, "py", None, ("grp", "px"), None),
        P(None, "py", None, ("grp", "px"), None),
        P(None, ("grp", "px"), None),
        P(None, ("grp", "px"), None),
    )
    return jax.shard_map(
        local,
        mesh=mesh,
        in_specs=placed,
        out_specs=(
            P(None, "py", None, ("grp", "px"), None),
            P(None, "py", None, ("grp", "px"), None),
        ),
        check_vma=False,
    )
```

profile of v0, /device:TPU:0, one launch (start us, length us, event | category | flops | bytes accessed | tf_op | source)
XLA Modules:
  0.0 775.5 jit_solution(9766000139064356499)
XLA Ops:
  0.6 22.9 %copy_subtract_fusion = f32[3,8,16,32,256]{4,2,1,3,0:T(8,128)S(1)} fusion(f32[3,8,16,32,256]{4,3,2,1,0:T(8,128)} %param.5, f32[3,8,16,32,256]{4,3,2,1,0:T(8,128)} %param.4), kind=kLoop, calls=%fused_computation.3 | loop fusion | flops 3145728 | bytes 37748736 | tf_op jit(solution)/shard_map/sub | solution.py:94
  25.7 5.8 collective-permute-start
  31.6 3.4 slice_bitcast_fusion.4
  36.1 2.6 slice_bitcast_fusion.2
  49.0 10.4 %fusion.4 = f32[1,8,16,32,256]{4,2,1,3,0:T(8,128)S(1)} fusion(f32[1,7,16,32,256]{4,2,1,3,0:T(8,128)} %slice_bitcast_fusion.7, f32[1,1,16,32,256]{4,2,1,3,0:T(8,128)} %bitcast.9, f32[1,8,16,31,256]{4,2,1,3,0:T(8,128)} %slice_bitcast_fusion.3, f32[1,8,16,1,256]{4,2,1,3,0:T(8,128)S(1)} %bitcast.104, f32[1,8,16,32,255]{4,2,1,3,0:T(8,128)} %slice_bitcast_fusion.2, ...), kind=kLoop, calls=%fused_computation.18 | loop fusion | flops 13631488 | bytes 30408720 | tf_op jit(solution)/shard_map/add | solution.py:107
  61.8 52.6 %all_to_all.66 = f32[1,8,16,32,256]{4,1,3,0,2:T(8,128)S(1)} all-to-all(f32[1,8,16,32,256]{4,1,3,0,2:T(8,128)S(1)} %copy.75), channel_id=1, replica_groups=mesh['grp'=2,'px'=4,'py'=4] {'grp','px'}, dimensions={2} | all-to-all | bytes 8388608 | tf_op jit(solution)/shard_map/all_to_all | solution.py:108
  115.7 4.8 fusion.42
  120.6 4.6 fusion.31
  125.2 5.4 copy.77
  130.6 4.9 all-to-all-start.1
  136.3 92.5 %all-to-all-done.1 = f32[1,8,2,256,256]{4,2,1,0,3:T(2,128)} async-done(((f32[1,8,2,256,256]{4,2,1,0,3:T(2,128)}), f32[1,8,2,256,256]{4,2,1,0,3:T(2,128)}, u32[]{:S(2)}, u32[]{:S(2)}) %all-to-all-start.1) | async-done | bytes 4194336 | tf_op jit(solution)/shard_map/all_to_all | solution.py:114
  228.8 6.0 fusion.6
  234.8 4.1 fusion.25
  238.9 4.1 fusion.28
  244.7 5.3 copy.80
  249.9 185.3 %all_to_all.67 = f32[2,32,2,64,256]{4,3,2,0,1:T(8,128)S(1)} all-to-all(f32[2,32,2,64,256]{4,3,2,0,1:T(8,128)S(1)} %copy.80), channel_id=1, replica_groups=mesh['grp'=2,'px'=4,'py'=4] {'py'}, dimensions={1} | all-to-all | bytes 16777216 | tf_op jit(solution)/shard_map/all_to_all | solution.py:125
  436.4 9.7 %fusion.45 = f32[256,2,8,2,256]{4,0,3,2,1:T(8,128)S(1)} fusion(f32[2,8,2,256,256]{4,3,2,1,0:T(8,128)S(1)} %bitcast.100), kind=kOutput, calls=%fused_computation.74 | convolution fusion | flops 6443499520 | bytes 16777216 | tf_op jit(solution)/shard_map/ctbxy,kx->ctbky/dot_general | solution.py:52
  446.1 8.2 %fusion = f32[2,8,2,256,256]{4,3,2,1,0:T(8,128)S(1)} fusion(f32[256,2,8,2,256]{4,0,3,2,1:T(8,128)S(1)} %fusion.45), kind=kOutput, calls=%fused_computation.7 | convolution fusion | flops 6443499520 | bytes 16777216 | tf_op jit(solution)/shard_map/ctbxy,ky->ctbxk/dot_general | solution.py:53
  454.5 3.1 copy-done.1
  457.8 3.1 slice_bitcast_fusion
  464.7 9.9 %fusion.104 = (f32[1,8,2,256,256]{4,3,2,1,0:T(8,128)S(1)}, f32[1,8,2,256,256]{4,3,2,1,0:T(8,128)}, f32[1,8,2,256,256]{4,3,2,1,0:T(8,128)}) fusion(f32[2,8,2,256,256]{4,3,2,1,0:T(8,128)} %copy-done.1, f32[1,8,2,1,256]{4,3,2,1,0:T(1,128)S(1)} %slice_bitcast_fusion.8, f32[1,8,2,255,256]{4,3,2,1,0:T(8,128)} %slice_bitcast_fusion.1, ...), kind=kLoop, calls=%fused_computation.143 | loop fusion | flops 4194304 | bytes 29360128 | tf_op jit(solution)/shard_map/slice | solution.py:132
  474.6 9.7 %pad_maximum_fusion = f32[3,8,2,256,256]{4,3,2,1,0:T(8,128)} fusion(f32[1,8,2,256,256]{4,3,2,1,0:T(8,128)} %get-tuple-element.21, f32[1,8,2,256,256]{4,3,2,1,0:T(8,128)} %get-tuple-element.20, f32[1,8,2,256,256]{4,3,2,1,0:T(8,128)S(1)} %get-tuple-element.19), kind=kLoop, calls=%fused_computation | loop fusion | flops 6291456 | bytes 25165824 | tf_op jit(solution)/shard_map/stack | solution.py:130
  484.3 21.0 %copy.85 = f32[3,8,2,256,256]{4,2,1,0,3:T(2,128)S(1)} copy(f32[3,8,2,256,256]{4,3,2,1,0:T(8,128)} %pad_maximum_fusion) | data formatting | bytes 25165824 | tf_op jit(solution)/shard_map/stack | solution.py:130
  505.3 143.1 %all_to_all.68 = f32[3,8,2,256,256]{4,2,1,0,3:T(2,128)S(1)} all-to-all(f32[3,8,2,256,256]{4,2,1,0,3:T(2,128)S(1)} %copy.85), channel_id=1, replica_groups=mesh['grp'=2,'px'=4,'py'=4] {'grp','px'}, dimensions={3} | all-to-all | bytes 25165824 | tf_op jit(solution)/shard_map/all_to_all | solution.py:137
  648.4 8.0 %copy.107 = f32[3,8,2,8,32,256]{5,2,3,1,4,0:T(2,128)} copy(f32[3,8,2,8,32,256]{5,2,1,0,4,3:T(2,128)S(1)} %bitcast.97) | data formatting | bytes 25165824 | tf_op jit(solution)/shard_map/all_to_all | solution.py:137
  656.4 15.7 %all_to_all.61 = f32[3,8,16,32,256]{4,2,1,3,0:T(8,128)} reshape(f32[3,8,8,2,32,256]{5,3,2,1,4,0:T(2,128)} %bitcast.98) | data formatting | bytes 25165824 | tf_op jit(solution)/shard_map/all_to_all | solution.py:137
  672.1 18.4 %copy_add_fusion = f32[3,8,16,32,256]{4,2,1,3,0:T(8,128)} fusion(f32[3,8,16,32,256]{4,2,1,3,0:T(8,128)} %all_to_all.61, f32[3,8,16,32,256]{4,3,2,1,0:T(8,128)} %param.4), kind=kLoop, calls=%fused_computation.5 | loop fusion | flops 3145728 | bytes 37748736 | tf_op jit(solution)/shard_map/add | solution.py:138
  690.5 14.7 %subtract_select_fusion = (f32[1,8,16,32,256]{4,2,1,3,0:T(8,128)}, f32[1,8,16,32,256]{4,2,1,3,0:T(8,128)S(1)}, pred[1,8,16,32,256]{4,2,1,3,0:T(8,128)(4,1)S(1)}) fusion(f32[3,8,16,32,256]{4,2,1,3,0:T(8,128)} %copy_add_fusion), kind=kLoop, calls=%fused_computation.11 | loop fusion | flops 55574528 | bytes 22020096 | tf_op jit(solution)/shard_map/jit(_where)/select_n | solution.py:82
  705.3 7.5 divide_select_fusion.1
  714.1 20.6 %pad_maximum_fusion.1 = (f32[3,8,16,32,256]{4,2,1,3,0:T(8,128)}, f32[3,8,16,32,256]{4,2,1,3,0:T(8,128)}) fusion(f32[1,8,16,32,256]{4,2,1,3,0:T(8,128)} %get-tuple-element.14, f32[1,8,16,32,256]{4,2,1,3,0:T(8,128)} %get-tuple-element.13, f32[1,8,16,32,256]{4,2,1,3,0:T(8,128)} %get-tuple-element.10, f32[3,8,16,32,256]{4,2,1,3,0:T(8,128)S(1)} %bitcast.96, ...), kind=kLoop, calls=%fused_computation.1 | loop fusion | flops 12582912 | bytes 62914560 | tf_op jit(solution)/shard_map/stack | solution.py:80
  734.8 20.2 %copy.90 = f32[3,8,16,32,256]{4,3,2,1,0:T(8,128)} copy(f32[3,8,16,32,256]{4,2,1,3,0:T(8,128)} %get-tuple-element.15) | data formatting | bytes 25165824
  754.9 20.4 %copy.89 = f32[3,8,16,32,256]{4,3,2,1,0:T(8,128)} copy(f32[3,8,16,32,256]{4,2,1,3,0:T(8,128)} %get-tuple-element.16) | data formatting | bytes 25165824
  (59 shorter events, 26.4 us)
Async XLA Ops:
  23.6 11.3 %copy-start = (f32[3,8,16,32,256]{4,2,1,3,0:T(8,128)}, f32[3,8,16,32,256]{4,2,1,3,0:T(8,128)S(1)}, u32[]{:S(2)}) copy-start(f32[3,8,16,32,256]{4,2,1,3,0:T(8,128)S(1)} %copy_subtract_fusion) | copy-start | bytes 37748740
  25.7 23.2 %collective-permute-start = (f32[1,16,32,256]{3,1,0,2:T(8,128)}, f32[1,16,32,256]{3,1,0,2:T(8,128)}, u32[]{:S(2)}, u32[]{:S(2)}) collective-permute-start(f32[1,16,32,256]{3,1,0,2:T(8,128)} %slice.83), channel_id=1, source_target_pairs={{0,1},{1,2},{2,3},{4,5},{5,6},{6,7},{8,9},{9,10},{10,11},{12,13},{... | collective-permute-start | bytes 1572872 | tf_op jit(solution)/shard_map/ppermute | solution.py:18
  35.8 13.1 %collective-permute-start.1 = (f32[8,16,1,256]{3,1,0,2:T(8,128)S(1)}, f32[8,16,1,256]{3,1,0,2:T(8,128)S(1)}, u32[]{:S(2)}, u32[]{:S(2)}) collective-permute-start(f32[8,16,1,256]{3,1,0,2:T(8,128)S(1)} %slice.86), channel_id=1, source_target_pairs={{28,0},{0,4},{4,8},{8,12},{12,16},{16,20},{20,24},{24,28},{29,1},{... | collective-permute-start | bytes 393224 | tf_op jit(solution)/shard_map/ppermute | solution.py:24
  36.1 3.7 copy-start.2
  42.3 2.8 copy-start.3
  44.5 1.0 copy-start.4
  130.6 98.2 %all-to-all-start.1 = ((f32[1,8,2,256,256]{4,2,1,0,3:T(2,128)}), f32[1,8,2,256,256]{4,2,1,0,3:T(2,128)}, u32[]{:S(2)}, u32[]{:S(2)}) async-start(f32[1,8,2,256,256]{4,2,1,0,3:T(2,128)} %copy.77), calls=%async_computation.1 | async-start | bytes 8388608 | tf_op jit(solution)/shard_map/all_to_all | solution.py:114
  454.2 3.4 copy-start.1
  690.5 22.3 %slice-start = ((s8[12582912]{0:T(1024)(128)(4,1)}), s8[4194304]{0:T(1024)(128)(4,1)S(1)}, s32[]{:S(2)}) async-start(s8[12582912]{0:T(1024)(128)(4,1)} %bitcast.93), calls=%async_computation.4 | async-start | bytes 8388608
  690.5 22.3 %slice-start.1 = ((s8[12582912]{0:T(1024)(128)(4,1)}), s8[4194304]{0:T(1024)(128)(4,1)S(1)}, s32[]{:S(2)}) async-start(s8[12582912]{0:T(1024)(128)(4,1)} %bitcast.93), calls=%async_computation.5 | async-start | bytes 8388608
  690.5 22.3 %slice-start.3 = ((s8[12582912]{0:T(1024)(128)(4,1)}), s8[4194304]{0:T(1024)(128)(4,1)S(1)}, s32[]{:S(2)}) async-start(s8[12582912]{0:T(1024)(128)(4,1)} %bitcast.95), calls=%async_computation.7 | async-start | bytes 8388608
  690.5 22.3 %slice-start.4 = ((s8[12582912]{0:T(1024)(128)(4,1)}), s8[4194304]{0:T(1024)(128)(4,1)S(1)}, s32[]{:S(2)}) async-start(s8[12582912]{0:T(1024)(128)(4,1)} %bitcast.95), calls=%async_computation.8 | async-start | bytes 8388608
  705.3 7.5 slice-start.2
  705.3 8.8 %slice-start.5 = ((s8[12582912]{0:T(1024)(128)(4,1)}), s8[4194304]{0:T(1024)(128)(4,1)S(1)}, s32[]{:S(2)}) async-start(s8[12582912]{0:T(1024)(128)(4,1)} %bitcast.95), calls=%async_computation.9 | async-start | bytes 8388608
where the time goes:
time: 783 us; the launch traced here: 776 us
  blocking collectives  381 us (49%)
  local copies, waits for them, and re-layouts  131 us (17%)
  other arithmetic  118 us (15%)
  waiting for transfers between devices  92.5 us (12%)
  matrix products  41.5 us (5%)
  starting transfers between devices  10.9 us (1%)
    all_to_all x1, blocking collectives, local(): lax.all_to_all(jnp.stack([potential, time_rate]), 'py', split_axis=1, con...  185 us
    all_to_all x1, blocking collectives, local(): lax.all_to_all(gradient, ('grp', 'px'), split_axis=3, concat_axis=2, tile...  143 us
    all_to_all x1, waiting for transfers between devices, local(): lax.all_to_all(spectral, 'py', split_axis=3, concat_axis=1, tiled=True)  92.5 us
    all_to_all x1, blocking collectives, local(): lax.all_to_all(payload, ('grp', 'px'), split_axis=2, concat_axis=3, tiled...  52.6 us
    unnamed x25, local copies, waits for them, and re-layouts  46.4 us
    all_to_all x2, local copies, waits for them, and re-layouts, local(): lax.all_to_all(gradient, ('grp', 'px'), split_axis=3, concat_axis=2, tile...  23.7 us
    sub x1, other arithmetic, local(): offset_field = auxiliary - multiplier / PENALTY  22.9 us
    another operation x1, local copies, waits for them, and re-layouts, local(): jnp.stack([space_values[1], jnp.roll(plane_potential, -1, axis=2) - plane...  21 us
  transfers between devices with their start and end apart: 3, of which 1 were waited for; matrix products, arithmetic and copies ran while one was open for 2% of the time, Pallas kernels for 0%

commit v1 on v0

v1 whole, which is shorter than its diff:
```python
import functools
import math

import jax
import jax.numpy as jnp
from jax import lax
from jax.experimental import pallas as pl
from jax.experimental.pallas import tpu as pltpu
from jax.sharding import PartitionSpec as P

NEWTON = 4
PENALTY = 1.0
PRECISE = lax.Precision.HIGHEST
VMEM_LIMIT = 60 * 1024 * 1024
SPACE = ("grp", "px")


def dot(a, b):
    return jnp.dot(a, b, precision=PRECISE, preferred_element_type=jnp.float32)


def hartley_table(length):
    row_index = lax.broadcasted_iota(jnp.int32, (length, length), 0)
    col_index = lax.broadcasted_iota(jnp.int32, (length, length), 1)
    phase_index = row_index * col_index % length
    angles = phase_index.astype(jnp.float32) * (2.0 * math.pi / length)
    return (jnp.cos(angles) + jnp.sin(angles)) / math.sqrt(length)


def mode_tables(rows, cols, here, blocks, block):
    m = lax.broadcasted_iota(jnp.int32, (rows, cols), 0)
    n = lax.broadcasted_iota(jnp.int32, (rows, cols), 1)
    m = jnp.minimum(m, rows - m).astype(jnp.float32)
    n = jnp.minimum(n, cols - n).astype(jnp.float32)
    lam = 4.0 * jnp.sin(m * (math.pi / rows)) ** 2 + 4.0 * jnp.sin(n * (math.pi / cols)) ** 2
    sinh = jnp.sqrt(lam * (1.0 + 0.25 * lam))
    inverse = 1.0 + 0.5 * lam + sinh
    ratio = 1.0 / inverse
    step = lax.integer_pow(ratio, here)
    double = step * step
    low = jnp.ones_like(step)
    high = jnp.ones_like(step)
    full = double
    for k in range(1, blocks):
        low = jnp.where(block >= k, low * double, low)
        high = jnp.where(blocks - 1 - block >= k, high * double, high)
        full = full * double
    positive = lam > 0.0
    scale = jnp.where(
        positive, 0.5 / jnp.where(positive, sinh * (1.0 - full), 1.0), 0.0
    )
    return jnp.stack([ratio, inverse, low, high, scale]), step


def source_kernel(mult, aux, start, end, table, out, prev, body, tail, *, levels):
    t = pl.program_id(0)
    here = pl.num_programs(0)
    problems, rows, cols = body.shape
    group, per = out.shape[0], out.shape[1]
    level = lax.axis_index("py") * here + t
    first = level == 0
    last = level == levels - 1

    @pl.when(t == 0)
    def _():
        prev[...] = jnp.zeros_like(prev)
        tail[...] = jnp.zeros_like(tail)

    row = lax.broadcasted_iota(jnp.int32, (rows, cols), 0)
    keep = jnp.where(last, 0.0, 1.0)
    begin = jnp.where(first, -1.0 / PENALTY, 0.0)
    finish = jnp.where(last, 1.0 / PENALTY, 0.0)

    def one(b, carry):
        along = aux[1, 0, b] - mult[1, 0, b] / PENALTY
        beside = jnp.where(row == 0, 0.0, pltpu.roll(along, 1, 0))
        second = aux[2, 0, b] - mult[2, 0, b] / PENALTY
        across = pltpu.roll(second, 1, 1) - second
        now = (aux[0, 0, b] - mult[0, 0, b] / PENALTY) * keep
        boundary = begin * start[b] + finish * end[b]
        body[b] = prev[b] - now + beside - along + across + boundary
        prev[b] = now
        tail[b, pl.ds(t, 1), :] = along[rows - 1 :, :]
        return carry

    lax.fori_loop(0, problems, one, 0)
    spread = dot(body[...].reshape(problems * rows, cols), table[...])
    at = pl.multiple_of(t * rows, rows)
    out[:, :, pl.ds(at, rows), :] = spread.reshape(group, per, rows, cols)

    @pl.when(t == here - 1)
    def _():
        beyond = dot(prev[...].reshape(problems * rows, cols), table[...])
        out[:, :, here * rows : here * rows + rows, :] = beyond.reshape(group, per, rows, cols)
        held = tail.shape[1]
        rims = dot(tail[...].reshape(problems * held, cols), table[...])
        out[:, :, here * rows + rows :, :] = rims.reshape(group, per, held, cols)


def forward_kernel(x, table, coef, modes, up, down, plane, *, here, rows):
    group = x.shape[0]
    total, cols = table.shape[0], x.shape[3]

    def one(t, carry):
        at = pl.multiple_of(t * rows, rows)
        plane[...] = x[:, 0, pl.ds(at, rows), :].reshape(total, cols)

        @pl.when(t < here)
        def _():
            for q in range(group):
                to = rows * ((q + 1) % group)
                plane[to : to + 1, :] += x[q, 0, pl.ds(here * rows + rows + t, 1), :]

        modes[0, t] = dot(table[...], plane[...])
        return carry

    lax.fori_loop(0, here + 1, one, 0)

    def sweep(c, carry):
        cut = pl.ds(pl.multiple_of(c * 8, 8), 8)
        ratio, inverse, low, high = (coef[k, cut, :] for k in range(4))
        square = ratio * ratio
        power = low * ratio
        total_up = jnp.zeros_like(ratio)
        for level in range(here + 1):
            total_up = ratio * total_up + (1.0 + power) * modes[0, level, cut, :]
            power = power * square
        up[0, cut, :] = total_up
        power = high * inverse
        total_down = jnp.zeros_like(ratio)
        for level in range(here, -1, -1):
            total_down = ratio * total_down + (1.0 + power) * modes[0, level, cut, :]
            power = power * square
        down[0, cut, :] = total_down
        return carry

    lax.fori_loop(0, total // 8, sweep, 0)


def backward_kernel(modes, up, down, table, coef, out, phi, *, here, rows, levels):
    group = out.shape[0]
    total, cols = table.shape[0], out.shape[3]

    def sweep(c, carry):
        cut = pl.ds(pl.multiple_of(c * 8, 8), 8)
        ratio, inverse, low, high, scale = (coef[k, cut, :] for k in range(5))
        square = ratio * ratio
        powers_low = []
        powers_high = []
        power = low * ratio
        for level in range(here + 1):
            powers_low.append(1.0 + power)
            power = power * square
        power = high * inverse
        for level in range(here + 1):
            powers_high.append(1.0 + power)
            power = power * square
        powers_high = powers_high[::-1]
        value = up[0, cut, :]
        for level in range(here + 1):
            if level:
                value = ratio * value
            value = value + powers_low[level] * modes[0, level, cut, :]
            phi[level, cut, :] = powers_high[level] * value
        behind = down[0, cut, :]
        for level in range(here, -1, -1):
            phi[level, cut, :] = scale * (phi[level, cut, :] + powers_low[level] * behind)
            behind = ratio * (behind + powers_high[level] * modes[0, level, cut, :])
        return carry

    lax.fori_loop(0, total // 8, sweep, 0)

    first = lax.axis_index("py") * here
    tile = (slice(0, 8), slice(0, 128))
    flat = (lax.broadcasted_iota(jnp.int32, (8, 128), 0) == 0) & (
        lax.broadcasted_iota(jnp.int32, (8, 128), 1) == 0
    )
    below = 0.5 * up[0, 0:8, 0:128]
    whole = below + 0.5 * down[0, 0:8, 0:128]
    for level in range(here + 1):
        whole = whole + modes[0, level, 0:8, 0:128]
    mean = whole * (1.0 / levels)
    value = jnp.zeros((8, 128), jnp.float32)
    for level in range(here + 1):
        phi[level, 0:8, 0:128] = jnp.where(flat, value, phi[level, 0:8, 0:128])
        if level < here:
            below = below + modes[0, level, 0:8, 0:128]
            count = (first + (level + 1)).astype(jnp.float32)
            value = value - (below - count * mean)

    if out.shape[2] > here * rows + rows + here:
        out[:, :, here * rows + rows :, :] = jnp.zeros(
            (group, 1, out.shape[2] - here * rows - rows, cols), jnp.float32
        )

    def one(t, carry):
        at = pl.multiple_of(t * rows, rows)
        field = dot(table[...], phi[t])
        out[:, 0, pl.ds(at, rows), :] = field.reshape(group, rows, cols)

        @pl.when(t < here)
        def _():
            for d in range(group):
                take = rows * ((d + 1) % group)
                out[d, 0, pl.ds(here * rows + rows + t, 1), :] = field[take : take + 1, :]

        return carry

    lax.fori_loop(0, here + 1, one, 0)


def project_kernel(
    x, mult, table, next_mult, next_aux, phi, following, rims, *, levels
):
    t = pl.program_id(0)
    here = pl.num_programs(0)
    problems, rows, cols = phi.shape
    held = rims.shape[1]
    level = lax.axis_index("py") * here + t
    moving = jnp.where(level == levels - 1, 0.0, 1.0)

    def field(at):
        flat = x[:, :, pl.ds(at, rows), :].reshape(problems * rows, cols)
        return dot(flat, table[...]).reshape(problems, rows, cols)

    @pl.when(t == 0)
    def _():
        following[...] = field(0)
        edge = x[:, :, here * rows + rows :, :].reshape(problems * held, cols)
        rims[...] = dot(edge, table[...]).reshape(problems, held, cols)

    phi[...] = following[...]
    following[...] = field(pl.multiple_of((t + 1) * rows, rows))
    row = lax.broadcasted_iota(jnp.int32, (rows, cols), 0)

    def one(b, carry):
        here_phi = phi[b]
        rim = jnp.broadcast_to(rims[b, pl.ds(t, 1), :], (rows, cols))
        grad_time = (following[b] - here_phi) * moving
        grad_first = jnp.where(row == rows - 1, rim, pltpu.roll(here_phi, rows - 1, 0)) - here_phi
        grad_second = pltpu.roll(here_phi, cols - 1, 1) - here_phi
        mult_time, mult_first, mult_second = (mult[k, 0, b] for k in range(3))
        time_part = grad_time + mult_time / PENALTY
        first = grad_first + mult_first / PENALTY
        second = grad_second + mult_second / PENALTY
        kinetic = 0.5 * (first * first + second * second)
        offset_one = 1.0 + time_part
        solid = kinetic > 1e-37
        root = jnp.exp(jnp.log(jnp.where(solid, kinetic, 1.0)) * (1.0 / 3.0))
        scaling = jnp.maximum(offset_one, 1.0) + jnp.where(solid, root, 0.0)
        for newton_step in range(NEWTON):
            residue = scaling * scaling * (scaling - offset_one) - kinetic
            derivative = scaling * (3.0 * scaling - 2.0 * offset_one)
            scaling = jnp.maximum(scaling - residue / derivative, 1.0)
        feasible = time_part + kinetic <= 0.0
        shrink = jnp.where(feasible, 1.0, 1.0 / scaling)
        out_time = jnp.where(feasible, time_part, time_part - (scaling - 1.0))
        out_first = first * shrink
        out_second = second * shrink
        next_aux[0, 0, b] = out_time
        next_aux[1, 0, b] = out_first
        next_aux[2, 0, b] = out_second
        next_mult[0, 0, b] = mult_time + PENALTY * (grad_time - out_time)
        next_mult[1, 0, b] = mult_first + PENALTY * (grad_first - out_first)
        next_mult[2, 0, b] = mult_second + PENALTY * (grad_second - out_second)
        return carry

    lax.fori_loop(0, problems, one, 0)


def params():
    return pltpu.CompilerParams(vmem_limit_bytes=VMEM_LIMIT)


def whole_block(shape):
    return pl.BlockSpec(shape, lambda *_: (0,) * len(shape))


def passed_along(value, steps):
    count = lax.axis_size("py")
    initial, last = (max(0, -steps), min(count, count - steps))
    return lax.ppermute(value, "py", [(k, k + steps) for k in range(initial, last)])


def local(multiplier, auxiliary, density_start, density_end):
    _, here, problems, rows, cols = multiplier.shape
    blocks = lax.axis_size("py")
    levels = here * blocks
    group = lax.axis_size("grp") * lax.axis_size("px")
    per = problems // group
    row_total = rows * group
    held = -(-here // 8) * 8
    packed = here * rows + rows + held
    f32 = jnp.float32
    table_cols = hartley_table(cols)
    table_rows = hartley_table(row_total)
    coef, step = mode_tables(row_total, cols, here, blocks, lax.axis_index("py"))

    level_block = pl.BlockSpec((3, 1, problems, rows, cols), lambda t: (0, t, 0, 0, 0))
    density_block = whole_block((problems, rows, cols))
    payload = pl.pallas_call(
        functools.partial(source_kernel, levels=levels),
        out_shape=jax.ShapeDtypeStruct((group, per, packed, cols), f32),
        grid=(here,),
        in_specs=[level_block, level_block, density_block, density_block, whole_block((cols, cols))],
        out_specs=whole_block((group, per, packed, cols)),
        scratch_shapes=[
            pltpu.VMEM((problems, rows, cols), f32),
            pltpu.VMEM((problems, rows, cols), f32),
            pltpu.VMEM((problems, held, cols), f32),
        ],
        compiler_params=params(),
        name="source",
    )(multiplier, auxiliary, density_start, density_end, table_cols)

    pencil = lax.all_to_all(payload, SPACE, split_axis=0, concat_axis=0, tiled=True)

    pencil_block = pl.BlockSpec((group, 1, packed, cols), lambda b: (0, b, 0, 0))
    modes_block = pl.BlockSpec((1, here + 1, row_total, cols), lambda b: (b, 0, 0, 0))
    carry_block = pl.BlockSpec((1, row_total, cols), lambda b: (b, 0, 0))
    carry_shape = jax.ShapeDtypeStruct((per, row_total, cols), f32)
    modes, up_own, down_own = pl.pallas_call(
        functools.partial(forward_kernel, here=here, rows=rows),
        out_shape=(
            jax.ShapeDtypeStruct((per, here + 1, row_total, cols), f32),
            carry_shape,
            carry_shape,
        ),
        grid=(per,),
        in_specs=[pencil_block, whole_block((row_total, row_total)), whole_block(coef.shape)],
        out_specs=(modes_block, carry_block, carry_block),
        scratch_shapes=[pltpu.VMEM((row_total, cols), f32)],
        compiler_params=params(),
        name="forward",
    )(pencil, table_rows, coef)

    up, down = up_own, down_own
    for hop in range(blocks - 1):
        up_in = passed_along(up, 1)
        down_in = passed_along(down, -1)
        up = up_own + step * up_in
        down = down_own + step * down_in

    returned = pl.pallas_call(
        functools.partial(backward_kernel, here=here, rows=rows, levels=levels),
        out_shape=jax.ShapeDtypeStruct((group, per, packed, cols), f32),
        grid=(per,),
        in_specs=[
            modes_block,
            carry_block,
            carry_block,
            whole_block((row_total, row_total)),
            whole_block(coef.shape),
        ],
        out_specs=pencil_block,
        scratch_shapes=[pltpu.VMEM((here + 1, row_total, cols), f32)],
        compiler_params=params(),
        name="backward",
    )(modes, up_in, down_in, table_rows, coef)

    slab = lax.all_to_all(returned, SPACE, split_axis=0, concat_axis=0, tiled=True)

    out_shape = jax.ShapeDtypeStruct(multiplier.shape, f32)
    return pl.pallas_call(
        functools.partial(project_kernel, levels=levels),
        out_shape=(out_shape, out_shape),
        grid=(here,),
        in_specs=[
            whole_block((group, per, packed, cols)),
            level_block,
            whole_block((cols, cols)),
        ],
        out_specs=(level_block, level_block),
        scratch_shapes=[
            pltpu.VMEM((problems, rows, cols), f32),
            pltpu.VMEM((problems, rows, cols), f32),
            pltpu.VMEM((problems, held, cols), f32),
        ],
        compiler_params=params(),
        name="project",
    )(slab, multiplier, table_cols)


def solution(mesh):
    placed = (
        P(None, "py", None, ("grp", "px"), None),
        P(None, "py", None, ("grp", "px"), None),
        P(None, ("grp", "px"), None),
        P(None, ("grp", "px"), None),
    )
    return jax.shard_map(
        local,
        mesh=mesh,
        in_specs=placed,
        out_specs=(
            P(None, "py", None, ("grp", "px"), None),
            P(None, "py", None, ("grp", "px"), None),
        ),
        check_vma=False,
    )
```

time: 783 us -> 258 us (0.33)
  blocking collectives: 381 us -> 60.9 us
  local copies, waits for them, and re-layouts: 131 us -> 0.8 us
  other arithmetic: 118 us -> 4.8 us
  Pallas kernels: 0 us -> 81.5 us
  matrix products: 41.5 us -> 0 us
  starting transfers between devices: 10.9 us -> 23 us
    all_to_all x3 -> x1, blocking collectives: 381 us -> 60.9 us  [local(): lax.all_to_all(returned, SPACE, split_axis=0, concat_axis=0, tiled=True)]
    pallas_call x0 -> x4, Pallas kernels: none -> 81.5 us  [the longest x1 33.8 us: local(): pl.pallas_call(functools.partial(project_kernel, levels=levels), out_shap...]
    unnamed x25 -> x10, local copies, waits for them, and re-layouts: 46.4 us -> 0.8 us
    dot_general x7 -> x0, matrix products: 41.5 us -> none  [the longest x2 14.5 us: spatial(): jnp.einsum('ctbxy,kx->ctbky', field, hartley_rows, precision=PRECISE)]
    all_to_all x1, waiting for transfers between devices: 92.5 us -> 53.9 us  [local(): lax.all_to_all(payload, SPACE, split_axis=0, concat_axis=0, tiled=True)]
    ppermute x2 -> x6, waiting for transfers between devices: 0.01 us -> 31.6 us  [passed_along(): lax.ppermute(value, 'py', [(k, k + steps) for k in range(initial, last)])]
    another operation x3 -> x1, other arithmetic: 31.9 us -> 0.33 us  [mode_tables(): return (jnp.stack([ratio, inverse, low, high, scale]), step)]
    add x4 -> x2, other arithmetic: 28.9 us -> 1.51 us  [local(): down = down_own + step * down_in]
  transfers between devices with their start and end apart: 3 -> 7, of which waited for: 1 -> 7; matrix products, arithmetic and copies ran while one was open for 2% -> 1% of each run, Pallas kernels for 0% -> 0%
where the time goes in v1:
time: 258 us; the launch traced here: 257 us
  waiting for transfers between devices  85.6 us (33%)
  Pallas kernels  81.5 us (32%)
  blocking collectives  60.9 us (24%)
  starting transfers between devices  23 us (9%)
  other arithmetic  4.8 us (2%)
    all_to_all x1, blocking collectives, local(): lax.all_to_all(returned, SPACE, split_axis=0, concat_axis=0, tiled=True)  60.9 us
    all_to_all x1, waiting for transfers between devices, local(): lax.all_to_all(payload, SPACE, split_axis=0, concat_axis=0, tiled=True)  53.9 us
    pallas_call x1, Pallas kernels, local(): pl.pallas_call(functools.partial(project_kernel, levels=levels), out_shap...  33.8 us
    ppermute x6, waiting for transfers between devices, passed_along(): lax.ppermute(value, 'py', [(k, k + steps) for k in range(initial, last)])  31.6 us
    pallas_call x1, Pallas kernels, local(): pl.pallas_call(functools.partial(source_kernel, levels=levels), out_shape...  20.7 us
    ppermute x6, starting transfers between devices, passed_along(): lax.ppermute(value, 'py', [(k, k + steps) for k in range(initial, last)])  17.8 us
    pallas_call x1, Pallas kernels, local(): pl.pallas_call(functools.partial(backward_kernel, here=here, rows=rows, l...  13.7 us
    pallas_call x1, Pallas kernels, local(): pl.pallas_call(functools.partial(forward_kernel, here=here, rows=rows), o...  13.3 us
  transfers between devices with their start and end apart: 7, of which 7 were waited for; matrix products, arithmetic and copies ran while one was open for 1% of the time, Pallas kernels for 0%

profile of v1, /device:TPU:0, one launch (start us, length us, event | category | flops | bytes accessed | tf_op | source)
XLA Modules:
  0.0 257.3 jit_solution(15264930103643053656)
XLA Ops:
  0.6 1.7 add_multiply_fusion.4.table
  2.4 20.7 %source.1 = f32[8,2,296,256]{3,2,1,0:T(8,128)} custom-call(f32[3,8,16,32,256]{4,3,2,1,0:T(8,128)} %mult.3, f32[3,8,16,32,256]{4,3,2,1,0:T(8,128)} %aux.1, f32[16,32,256]{2,1,0:T(8,128)} %start.1, f32[16,32,256]{2,1,0:T(8,128)} %end.1, f32[256,256]{1,0:T(8,128)} %add_multiply_fusion.4.table), custom_call_target="tpu_custom_call" | custom-call | tf_op jit(solution)/shard_map/source/pallas_call | solution.py:301
  23.1 5.2 %all-to-all-start = ((f32[8,2,296,256]{3,2,1,0:T(8,128)}), f32[8,2,296,256]{3,2,1,0:T(8,128)}, u32[]{:S(2)}, u32[]{:S(2)}) async-start(f32[8,2,296,256]{3,2,1,0:T(8,128)} %source.1), calls=%async_computation | async-start | bytes 9699328 | tf_op jit(solution)/shard_map/all_to_all | solution.py:316
  28.3 0.2 fusion.29
  28.5 0.2 fusion.27
  28.7 0.3 fusion.6
  29.0 0.3 fusion.7
  29.3 0.3 fusion.13.coef
  29.7 53.9 %all-to-all-done.x = f32[8,2,296,256]{3,2,1,0:T(8,128)} async-done(((f32[8,2,296,256]{3,2,1,0:T(8,128)}), f32[8,2,296,256]{3,2,1,0:T(8,128)}, u32[]{:S(2)}, u32[]{:S(2)}) %all-to-all-start) | async-done | bytes 4849696 | tf_op jit(solution)/shard_map/all_to_all | solution.py:316
  83.6 0.0 copy-done
  83.6 13.3 %forward.1 = (f32[2,9,256,256]{3,2,1,0:T(8,128)}, f32[2,256,256]{2,1,0:T(8,128)}, f32[2,256,256]{2,1,0:T(8,128)}) custom-call(f32[8,2,296,256]{3,2,1,0:T(8,128)} %all-to-all-done.x, f32[256,256]{1,0:T(8,128)} %add_multiply_fusion.4.table, f32[5,256,256]{2,1,0:T(8,128)} %copy-done), custom_call_target="tpu_custom_call" | custom-call | tf_op jit(solution)/shard_map/forward/pallas_call | solution.py:322
  96.9 4.3 %collective-permute-start = (f32[2,256,256]{2,1,0:T(8,128)}, f32[2,256,256]{2,1,0:T(8,128)S(1)}, u32[]{:S(2)}, u32[]{:S(2)}) collective-permute-start(f32[2,256,256]{2,1,0:T(8,128)} %get-tuple-element.6), channel_id=1, source_target_pairs={{0,1},{1,2},{2,3},{4,5},{5,6},{6,7},{8,9},{9,10},{10,11},{12,13},{... | collective-permute-start | bytes 1572872 | tf_op jit(solution)/shard_map/ppermute | solution.py:282
  101.2 1.3 collective-permute-start.3
  102.5 0.2 fusion.21
  102.7 0.0 copy-start.1
  102.8 0.0 copy-start.2
  102.8 9.6 %collective-permute-done = f32[2,256,256]{2,1,0:T(8,128)S(1)} collective-permute-done((f32[2,256,256]{2,1,0:T(8,128)}, f32[2,256,256]{2,1,0:T(8,128)S(1)}, u32[]{:S(2)}, u32[]{:S(2)}) %collective-permute-start) | collective-permute-done | bytes 524320 | tf_op jit(solution)/shard_map/ppermute | solution.py:282
  112.4 4.0 %collective-permute-done.3 = f32[2,256,256]{2,1,0:T(8,128)S(1)} collective-permute-done((f32[2,256,256]{2,1,0:T(8,128)}, f32[2,256,256]{2,1,0:T(8,128)S(1)}, u32[]{:S(2)}, u32[]{:S(2)}) %collective-permute-start.3) | collective-permute-done | bytes 524320 | tf_op jit(solution)/shard_map/ppermute | solution.py:282
  116.4 1.4 multiply_add_fusion.1
  117.8 1.3 collective-permute-start.4
  119.1 4.6 %collective-permute-start.1 = (f32[2,256,256]{2,1,0:T(8,128)S(1)}, f32[2,256,256]{2,1,0:T(8,128)S(1)}, u32[]{:S(2)}, u32[]{:S(2)}) collective-permute-start(f32[2,256,256]{2,1,0:T(8,128)S(1)} %get-tuple-element.11), channel_id=1, source_target_pairs={{0,1},{1,2},{2,3},{4,5},{5,6},{6,7},{8,9},{9,10},{10,11},{12,13},{... | collective-permute-start | bytes 1572872 | tf_op jit(solution)/shard_map/ppermute | solution.py:282
  123.7 8.2 %collective-permute-done.4 = f32[2,256,256]{2,1,0:T(8,128)S(1)} collective-permute-done((f32[2,256,256]{2,1,0:T(8,128)S(1)}, f32[2,256,256]{2,1,0:T(8,128)S(1)}, u32[]{:S(2)}, u32[]{:S(2)}) %collective-permute-start.4) | collective-permute-done | bytes 524320 | tf_op jit(solution)/shard_map/ppermute | solution.py:282
  131.9 1.2 collective-permute-done.1
  133.1 0.2 multiply_add_fusion
  133.2 1.3 collective-permute-start.5
  134.5 5.0 %collective-permute-start.2 = (f32[2,256,256]{2,1,0:T(8,128)S(1)}, f32[2,256,256]{2,1,0:T(8,128)S(1)}, u32[]{:S(2)}, u32[]{:S(2)}) collective-permute-start(f32[2,256,256]{2,1,0:T(8,128)S(1)} %get-tuple-element.9), channel_id=1, source_target_pairs={{0,1},{1,2},{2,3},{4,5},{5,6},{6,7},{8,9},{9,10},{10,11},{12,13},{... | collective-permute-start | bytes 1572872 | tf_op jit(solution)/shard_map/ppermute | solution.py:282
  139.6 7.4 %collective-permute-done.5.down = f32[2,256,256]{2,1,0:T(8,128)S(1)} collective-permute-done((f32[2,256,256]{2,1,0:T(8,128)S(1)}, f32[2,256,256]{2,1,0:T(8,128)S(1)}, u32[]{:S(2)}, u32[]{:S(2)}) %collective-permute-start.5) | collective-permute-done | bytes 524320 | tf_op jit(solution)/shard_map/ppermute | solution.py:282
  147.0 1.2 collective-permute-done.2.up
  148.2 0.8 copy-done.4
  149.0 13.7 %backward.1 = f32[8,2,296,256]{3,2,1,0:T(8,128)} custom-call(f32[2,9,256,256]{3,2,1,0:T(8,128)} %get-tuple-element.5.modes, f32[2,256,256]{2,1,0:T(8,128)} %copy-done.4, f32[2,256,256]{2,1,0:T(8,128)} %copy-done.3, f32[256,256]{1,0:T(8,128)} %add_multiply_fusion.4.table, f32[5,256,256]{2,1,0:T(8,128)} %copy-done), custom_call_target="tpu_custom_call" | custom-call | tf_op jit(solution)/shard_map/backward/pallas_call | solution.py:344
  162.6 60.9 %all_to_all.10.x = f32[8,2,296,256]{3,2,1,0:T(8,128)} all-to-all(f32[8,2,296,256]{3,2,1,0:T(8,128)} %backward.1), channel_id=1, replica_groups=mesh['grp'=2,'px'=4,'py'=4] {'grp','px'}, dimensions={0} | all-to-all | bytes 9699328 | tf_op jit(solution)/shard_map/all_to_all | solution.py:361
  223.5 33.8 %project.1 = (f32[3,8,16,32,256]{4,3,2,1,0:T(8,128)}, f32[3,8,16,32,256]{4,3,2,1,0:T(8,128)}) custom-call(f32[8,2,296,256]{3,2,1,0:T(8,128)} %all_to_all.10.x, f32[3,8,16,32,256]{4,3,2,1,0:T(8,128)} %mult.3, f32[256,256]{1,0:T(8,128)} %add_multiply_fusion.4.table), custom_call_target="tpu_custom_call" | custom-call | tf_op jit(solution)/shard_map/project/pallas_call | solution.py:364
  (7 shorter events, 0.1 us)
Async XLA Ops:
  23.1 60.5 %all-to-all-start = ((f32[8,2,296,256]{3,2,1,0:T(8,128)}), f32[8,2,296,256]{3,2,1,0:T(8,128)}, u32[]{:S(2)}, u32[]{:S(2)}) async-start(f32[8,2,296,256]{3,2,1,0:T(8,128)} %source.1), calls=%async_computation | async-start | bytes 9699328 | tf_op jit(solution)/shard_map/all_to_all | solution.py:316
  29.7 53.9 %copy-start = (f32[5,256,256]{2,1,0:T(8,128)}, f32[5,256,256]{2,1,0:T(8,128)S(1)}, u32[]{:S(2)}) copy-start(f32[5,256,256]{2,1,0:T(8,128)S(1)} %fusion.13.coef) | copy-start | bytes 3932164
  96.9 15.5 %collective-permute-start = (f32[2,256,256]{2,1,0:T(8,128)}, f32[2,256,256]{2,1,0:T(8,128)S(1)}, u32[]{:S(2)}, u32[]{:S(2)}) collective-permute-start(f32[2,256,256]{2,1,0:T(8,128)} %get-tuple-element.6), channel_id=1, source_target_pairs={{0,1},{1,2},{2,3},{4,5},{5,6},{6,7},{8,9},{9,10},{10,11},{12,13},{... | collective-permute-start | bytes 1572872 | tf_op jit(solution)/shard_map/ppermute | solution.py:282
  101.2 15.2 %collective-permute-start.3 = (f32[2,256,256]{2,1,0:T(8,128)}, f32[2,256,256]{2,1,0:T(8,128)S(1)}, u32[]{:S(2)}, u32[]{:S(2)}) collective-permute-start(f32[2,256,256]{2,1,0:T(8,128)} %get-tuple-element.7), channel_id=1, source_target_pairs={{1,0},{2,1},{3,2},{5,4},{6,5},{7,6},{9,8},{10,9},{11,10},{13,12},{... | collective-permute-start | bytes 1572872 | tf_op jit(solution)/shard_map/ppermute | solution.py:282
  102.7 30.3 %copy-start.1 = (f32[2,256,256]{2,1,0:T(8,128)S(1)}, f32[2,256,256]{2,1,0:T(8,128)}, u32[]{:S(2)}) copy-start(f32[2,256,256]{2,1,0:T(8,128)} %get-tuple-element.6) | copy-start | bytes 1572868
  102.8 30.3 %copy-start.2 = (f32[2,256,256]{2,1,0:T(8,128)S(1)}, f32[2,256,256]{2,1,0:T(8,128)}, u32[]{:S(2)}) copy-start(f32[2,256,256]{2,1,0:T(8,128)} %get-tuple-element.7) | copy-start | bytes 1572868
  117.8 14.1 %collective-permute-start.4 = (f32[2,256,256]{2,1,0:T(8,128)S(1)}, f32[2,256,256]{2,1,0:T(8,128)S(1)}, u32[]{:S(2)}, u32[]{:S(2)}) collective-permute-start(f32[2,256,256]{2,1,0:T(8,128)S(1)} %get-tuple-element.10), channel_id=1, source_target_pairs={{1,0},{2,1},{3,2},{5,4},{6,5},{7,6},{9,8},{10,9},{11,10},{13,12},{... | collective-permute-start | bytes 1572872 | tf_op jit(solution)/shard_map/ppermute | solution.py:282
  119.1 14.0 %collective-permute-start.1 = (f32[2,256,256]{2,1,0:T(8,128)S(1)}, f32[2,256,256]{2,1,0:T(8,128)S(1)}, u32[]{:S(2)}, u32[]{:S(2)}) collective-permute-start(f32[2,256,256]{2,1,0:T(8,128)S(1)} %get-tuple-element.11), channel_id=1, source_target_pairs={{0,1},{1,2},{2,3},{4,5},{5,6},{6,7},{8,9},{9,10},{10,11},{12,13},{... | collective-permute-start | bytes 1572872 | tf_op jit(solution)/shard_map/ppermute | solution.py:282
  133.2 13.7 %collective-permute-start.5 = (f32[2,256,256]{2,1,0:T(8,128)S(1)}, f32[2,256,256]{2,1,0:T(8,128)S(1)}, u32[]{:S(2)}, u32[]{:S(2)}) collective-permute-start(f32[2,256,256]{2,1,0:T(8,128)S(1)} %get-tuple-element.8), channel_id=1, source_target_pairs={{1,0},{2,1},{3,2},{5,4},{6,5},{7,6},{9,8},{10,9},{11,10},{13,12},{... | collective-permute-start | bytes 1572872 | tf_op jit(solution)/shard_map/ppermute | solution.py:282
  134.5 13.6 %collective-permute-start.2 = (f32[2,256,256]{2,1,0:T(8,128)S(1)}, f32[2,256,256]{2,1,0:T(8,128)S(1)}, u32[]{:S(2)}, u32[]{:S(2)}) collective-permute-start(f32[2,256,256]{2,1,0:T(8,128)S(1)} %get-tuple-element.9), channel_id=1, source_target_pairs={{0,1},{1,2},{2,3},{4,5},{5,6},{6,7},{8,9},{9,10},{10,11},{12,13},{... | collective-permute-start | bytes 1572872 | tf_op jit(solution)/shard_map/ppermute | solution.py:282
  147.0 1.2 copy-start.3
  148.2 0.8 copy-start.4

commit v2 on v1

--- a/solution.py
+++ b/solution.py
@@ -135,6 +135,114 @@
         return carry
 
     lax.fori_loop(0, total // 8, sweep, 0)
+
+
+def carry_kernel(up_own, down_own, step, up_in, down_in, up_got, down_got, up_out, down_out,
+                 up_sent, up_came, down_sent, down_came, *, blocks, pieces, lag):
+    me = lax.axis_index("py")
+    size = up_own.shape[1] // pieces
+    has_lower = me > 0
+    has_upper = me < blocks - 1
+    pairs = [(b, c) for b in range(up_own.shape[0]) for c in range(pieces)]
+
+    def copy(source, target, sent, came, k, other):
+        b, c = pairs[k]
+        cut = pl.ds(c * size, size)
+        return pltpu.make_async_remote_copy(
+            src_ref=source.at[b, cut, :],
+            dst_ref=target.at[b, cut, :],
+            send_sem=sent.at[k],
+            recv_sem=came.at[k],
+            device_id={"py": other},
+            device_id_type=pl.DeviceIdType.MESH,
+        )
+
+    barrier = pltpu.get_barrier_semaphore()
+
+    @pl.when(has_lower)
+    def _():
+        pl.semaphore_signal(
+            barrier, inc=1, device_id={"py": me - 1}, device_id_type=pl.DeviceIdType.MESH
+        )
+
+    @pl.when(has_upper)
+    def _():
+        pl.semaphore_signal(
+            barrier, inc=1, device_id={"py": me + 1}, device_id_type=pl.DeviceIdType.MESH
+        )
+
+    @pl.when(has_lower & has_upper)
+    def _():
+        pl.semaphore_wait(barrier, 2)
+
+    @pl.when(jnp.logical_not(has_lower & has_upper))
+    def _():
+        pl.semaphore_wait(barrier, 1)
+
+    def relay(k, own, got, out, sent, came, first, last, ahead):
+        b, c = pairs[k]
+        cut = pl.ds(c * size, size)
+
+        @pl.when(jnp.logical_not(first))
+        def _():
+            copy(out, got, sent, came, k, ahead).wait_recv()
+
+            @pl.when(jnp.logical_not(last))
+            def _():
+                out[b, cut, :] = own[b, cut, :] + step[cut, :] * got[b, cut, :]
+                copy(out, got, sent, came, k, ahead).start()
+
+    up = (up_own, up_got, up_out, up_sent, up_came, me == 0, me == blocks - 1,
+          (me + 1) % blocks)
+    down = (down_own, down_got, down_out, down_sent, down_came, me == blocks - 1, me == 0,
+            (me + blocks - 1) % blocks)
+
+    @pl.when(me == 0)
+    def _():
+        for k in range(len(pairs)):
+            copy(up_own, up_got, up_sent, up_came, k, me + 1).start()
+
+    @pl.when(me == blocks - 1)
+    def _():
+        for k in range(len(pairs)):
+            copy(down_own, down_got, down_sent, down_came, k, me - 1).start()
+
+    def weave(early, late):
+        for k in range(len(pairs) + lag):
+            if k < len(pairs):
+                relay(k, *early)
+            if k >= lag:
+                relay(k - lag, *late)
+
+    lower_half = me < blocks // 2
+
+    @pl.when(lower_half)
+    def _():
+        weave(up, down)
+
+    @pl.when(jnp.logical_not(lower_half))
+    def _():
+        weave(down, up)
+
+    @pl.when(has_lower)
+    def _():
+        up_in[...] = up_got[...]
+        for k in range(len(pairs)):
+            copy(down_out, down_got, down_sent, down_came, k, me - 1).wait_send()
+
+    @pl.when(me == 0)
+    def _():
+        up_in[...] = jnp.zeros_like(up_in)
+
+    @pl.when(has_upper)
+    def _():
+        down_in[...] = down_got[...]
+        for k in range(len(pairs)):
+            copy(up_out, up_got, up_sent, up_came, k, me + 1).wait_send()
+
+    @pl.when(me == blocks - 1)
+    def _():
+        down_in[...] = jnp.zeros_like(down_in)
 
 
 def backward_kernel(modes, up, down, table, coef, out, phi, *, here, rows, levels):
@@ -276,12 +384,6 @@
     return pl.BlockSpec(shape, lambda *_: (0,) * len(shape))
 
 
-def passed_along(value, steps):
-    count = lax.axis_size("py")
-    initial, last = (max(0, -steps), min(count, count - steps))
-    return lax.ppermute(value, "py", [(k, k + steps) for k in range(initial, last)])
-
-
 def local(multiplier, auxiliary, density_start, density_end):
     _, here, problems, rows, cols = multiplier.shape
     blocks = lax.axis_size("py")
@@ -334,12 +436,21 @@
         name="forward",
     )(pencil, table_rows, coef)
 
-    up, down = up_own, down_own
-    for hop in range(blocks - 1):
-        up_in = passed_along(up, 1)
-        down_in = passed_along(down, -1)
-        up = up_own + step * up_in
-        down = down_own + step * down_in
+    pieces = math.gcd(row_total // 8, 4)
+    count = per * pieces
+    vmem = pl.BlockSpec(memory_space=pltpu.VMEM)
+    up_in, down_in = pl.pallas_call(
+        functools.partial(carry_kernel, blocks=blocks, pieces=pieces, lag=min(3, count)),
+        out_shape=(carry_shape, carry_shape),
+        in_specs=[vmem, vmem, vmem],
+        out_specs=(vmem, vmem),
+        scratch_shapes=[pltpu.VMEM((per, row_total, cols), f32)] * 4
+        + [pltpu.SemaphoreType.DMA((count,))] * 4,
+        compiler_params=pltpu.CompilerParams(
+            collective_id=0, has_side_effects=True, vmem_limit_bytes=24 * 1024 * 1024
+        ),
+        name="carry",
+    )(up_own, down_own, step)
 
     returned = pl.pallas_call(
         functools.partial(backward_kernel, here=here, rows=rows, levels=levels),

time: 258 us -> 232 us (0.90)
  waiting for transfers between devices: 85.6 us -> 53.7 us
  Pallas kernels: 81.5 us -> 104 us
  starting transfers between devices: 23 us -> 5.17 us
  local copies, waits for them, and re-layouts: 0.8 us -> 3.68 us
    ppermute x6 -> x0, waiting for transfers between devices: 31.6 us -> none  [passed_along(): lax.ppermute(value, 'py', [(k, k + steps) for k in range(initial, last)])]
    pallas_call x0 -> x1, Pallas kernels: none -> 22.7 us  [local(): pl.pallas_call(functools.partial(carry_kernel, blocks=blocks, pieces=piec...]
    ppermute x6 -> x0, starting transfers between devices: 17.8 us -> none  [passed_along(): lax.ppermute(value, 'py', [(k, k + steps) for k in range(initial, last)])]
    unnamed x10, local copies, waits for them, and re-layouts: 0.8 us -> 3.68 us
  transfers between devices with their start and end apart: 7 -> 1, of which waited for: 7 -> 1; matrix products, arithmetic and copies ran while one was open for 1% -> 1% of each run, Pallas kernels for 0% -> 0%
where the time goes in v2:
time: 232 us
  Pallas kernels  104 us (45%)
  blocking collectives  60.9 us (26%)
  waiting for transfers between devices  53.7 us (23%)
  starting transfers between devices  5.17 us (2%)
  local copies, waits for them, and re-layouts  3.68 us (2%)
  other arithmetic  3.3 us (1%)
    all_to_all x1, blocking collectives, local(): lax.all_to_all(returned, SPACE, split_axis=0, concat_axis=0, tiled=True)  60.9 us
    all_to_all x1, waiting for transfers between devices, local(): lax.all_to_all(payload, SPACE, split_axis=0, concat_axis=0, tiled=True)  53.7 us
    pallas_call x1, Pallas kernels, local(): pl.pallas_call(functools.partial(project_kernel, levels=levels), out_shap...  33.8 us
    pallas_call x1, Pallas kernels, local(): pl.pallas_call(functools.partial(carry_kernel, blocks=blocks, pieces=piec...  22.7 us
    pallas_call x1, Pallas kernels, local(): pl.pallas_call(functools.partial(source_kernel, levels=levels), out_shape...  20.7 us
    pallas_call x1, Pallas kernels, local(): pl.pallas_call(functools.partial(backward_kernel, here=here, rows=rows, l...  13.7 us
    pallas_call x1, Pallas kernels, local(): pl.pallas_call(functools.partial(forward_kernel, here=here, rows=rows), o...  13.3 us
    all_to_all x1, starting transfers between devices, local(): lax.all_to_all(payload, SPACE, split_axis=0, concat_axis=0, tiled=True)  5.17 us
  transfers between devices with their start and end apart: 1, of which 1 were waited for; matrix products, arithmetic and copies ran while one was open for 1% of the time, Pallas kernels for 0%

profile of v2, /device:TPU:0, one launch (start us, length us, event | category | flops | bytes accessed | tf_op | source)
XLA Modules:
  0.0 231.7 jit_solution(8730100430547312171)
XLA Ops:
  0.6 1.7 add_multiply_fusion.4.table
  2.4 20.7 %source.1 = f32[8,2,296,256]{3,2,1,0:T(8,128)} custom-call(f32[3,8,16,32,256]{4,3,2,1,0:T(8,128)} %mult.3, f32[3,8,16,32,256]{4,3,2,1,0:T(8,128)} %aux.1, f32[16,32,256]{2,1,0:T(8,128)} %start.1, f32[16,32,256]{2,1,0:T(8,128)} %end.1, f32[256,256]{1,0:T(8,128)} %add_multiply_fusion.4.table), custom_call_target="tpu_custom_call" | custom-call | tf_op jit(solution)/shard_map/source/pallas_call | solution.py:403
  23.1 5.2 %all-to-all-start = ((f32[8,2,296,256]{3,2,1,0:T(8,128)}), f32[8,2,296,256]{3,2,1,0:T(8,128)}, u32[]{:S(2)}, u32[]{:S(2)}) async-start(f32[8,2,296,256]{3,2,1,0:T(8,128)} %source.1), calls=%async_computation | async-start | bytes 9699328 | tf_op jit(solution)/shard_map/all_to_all | solution.py:418
  28.3 0.2 fusion.21.step
  28.6 0.2 fusion.29
  28.8 0.2 fusion.27
  29.0 0.3 fusion.6
  29.2 0.3 fusion.7
  29.5 0.3 fusion.13.coef
  29.9 0.0 copy-start.4
  29.9 53.7 %all-to-all-done.x = f32[8,2,296,256]{3,2,1,0:T(8,128)} async-done(((f32[8,2,296,256]{3,2,1,0:T(8,128)}), f32[8,2,296,256]{3,2,1,0:T(8,128)}, u32[]{:S(2)}, u32[]{:S(2)}) %all-to-all-start) | async-done | bytes 4849696 | tf_op jit(solution)/shard_map/all_to_all | solution.py:418
  83.6 0.0 copy-done.4
  83.6 13.3 %forward.1 = (f32[2,9,256,256]{3,2,1,0:T(8,128)}, f32[2,256,256]{2,1,0:T(8,128)}, f32[2,256,256]{2,1,0:T(8,128)}) custom-call(f32[8,2,296,256]{3,2,1,0:T(8,128)} %all-to-all-done.x, f32[256,256]{1,0:T(8,128)} %add_multiply_fusion.4.table, f32[5,256,256]{2,1,0:T(8,128)} %copy-done.4), custom_call_target="tpu_custom_call" | custom-call | tf_op jit(solution)/shard_map/forward/pallas_call | solution.py:424
  96.9 0.0 copy-start.2
  96.9 1.0 copy-done.2
  97.9 0.0 copy-start.3
  97.9 1.0 copy-done.3
  99.0 22.7 %carry.1 = (f32[2,256,256]{2,1,0:T(8,128)S(1)}, f32[2,256,256]{2,1,0:T(8,128)S(1)}) custom-call(f32[2,256,256]{2,1,0:T(8,128)S(1)} %copy-done.2, f32[2,256,256]{2,1,0:T(8,128)S(1)} %copy-done.3, f32[256,256]{1,0:T(8,128)S(1)} %fusion.21.step), custom_call_target="tpu_custom_call" | custom-call | tf_op jit(solution)/shard_map/carry/pallas_call | solution.py:442
  121.7 0.0 copy-start
  121.7 0.8 copy-done
  122.5 0.0 copy-start.1
  122.5 0.8 copy-done.1
  123.3 13.7 %backward.1 = f32[8,2,296,256]{3,2,1,0:T(8,128)} custom-call(f32[2,9,256,256]{3,2,1,0:T(8,128)} %get-tuple-element.7.modes, f32[2,256,256]{2,1,0:T(8,128)} %copy-done, f32[2,256,256]{2,1,0:T(8,128)} %copy-done.1, f32[256,256]{1,0:T(8,128)} %add_multiply_fusion.4.table, f32[5,256,256]{2,1,0:T(8,128)} %copy-done.4), custom_call_target="tpu_custom_call" | custom-call | tf_op jit(solution)/shard_map/backward/pallas_call | solution.py:455
  137.0 60.9 %all_to_all.10.x = f32[8,2,296,256]{3,2,1,0:T(8,128)} all-to-all(f32[8,2,296,256]{3,2,1,0:T(8,128)} %backward.1), channel_id=1, replica_groups=mesh['grp'=2,'px'=4,'py'=4] {'grp','px'}, dimensions={0} | all-to-all | bytes 9699328 | tf_op jit(solution)/shard_map/all_to_all | solution.py:472
  197.9 33.8 %project.1 = (f32[3,8,16,32,256]{4,3,2,1,0:T(8,128)}, f32[3,8,16,32,256]{4,3,2,1,0:T(8,128)}) custom-call(f32[8,2,296,256]{3,2,1,0:T(8,128)} %all_to_all.10.x, f32[3,8,16,32,256]{4,3,2,1,0:T(8,128)} %mult.3, f32[256,256]{1,0:T(8,128)} %add_multiply_fusion.4.table), custom_call_target="tpu_custom_call" | custom-call | tf_op jit(solution)/shard_map/project/pallas_call | solution.py:475
  (1 shorter events, 0.0 us)
Async XLA Ops:
  23.1 60.5 %all-to-all-start = ((f32[8,2,296,256]{3,2,1,0:T(8,128)}), f32[8,2,296,256]{3,2,1,0:T(8,128)}, u32[]{:S(2)}, u32[]{:S(2)}) async-start(f32[8,2,296,256]{3,2,1,0:T(8,128)} %source.1), calls=%async_computation | async-start | bytes 9699328 | tf_op jit(solution)/shard_map/all_to_all | solution.py:418
  29.9 53.7 %copy-start.4 = (f32[5,256,256]{2,1,0:T(8,128)}, f32[5,256,256]{2,1,0:T(8,128)S(1)}, u32[]{:S(2)}) copy-start(f32[5,256,256]{2,1,0:T(8,128)S(1)} %fusion.13.coef) | copy-start | bytes 3932164
  96.9 1.0 copy-start.2
  97.9 1.0 copy-start.3
  121.7 0.8 copy-start
  122.5 0.8 copy-start.1

commit v3 on v2

--- a/solution.py
+++ b/solution.py
@@ -83,7 +83,7 @@
         tail[b, pl.ds(t, 1), :] = along[rows - 1 :, :]
         return carry
 
-    lax.fori_loop(0, problems, one, 0)
+    lax.fori_loop(0, problems, one, 0, unroll=4)
     spread = dot(body[...].reshape(problems * rows, cols), table[...])
     at = pl.multiple_of(t * rows, rows)
     out[:, :, pl.ds(at, rows), :] = spread.reshape(group, per, rows, cols)
@@ -134,7 +134,7 @@
         down[0, cut, :] = total_down
         return carry
 
-    lax.fori_loop(0, total // 8, sweep, 0)
+    lax.fori_loop(0, total // 8, sweep, 0, unroll=4)
 
 
 def carry_kernel(up_own, down_own, step, up_in, down_in, up_got, down_got, up_out, down_out,
@@ -276,7 +276,7 @@
             behind = ratio * (behind + powers_high[level] * modes[0, level, cut, :])
         return carry
 
-    lax.fori_loop(0, total // 8, sweep, 0)
+    lax.fori_loop(0, total // 8, sweep, 0, unroll=4)
 
     first = lax.axis_index("py") * here
     tile = (slice(0, 8), slice(0, 128))
@@ -373,7 +373,7 @@
         next_mult[2, 0, b] = mult_second + PENALTY * (grad_second - out_second)
         return carry
 
-    lax.fori_loop(0, problems, one, 0)
+    lax.fori_loop(0, problems, one, 0, unroll=2)
 
 
 def params():

time: 232 us -> 222 us (0.957)
  Pallas kernels: 104 us -> 93.8 us
    pallas_call x1, Pallas kernels: 33.8 us -> 28.4 us  [local(): pl.pallas_call(functools.partial(project_kernel, levels=levels), out_shap...]
    pallas_call x1, Pallas kernels: 20.7 us -> 16.6 us  [local(): pl.pallas_call(functools.partial(source_kernel, levels=levels), out_shape...]
where the time goes in v3:
time: 222 us; the launch traced here: 221 us
  Pallas kernels  93.8 us (42%)
  blocking collectives  60.9 us (27%)
  waiting for transfers between devices  53.7 us (24%)
  starting transfers between devices  5.19 us (2%)
  local copies, waits for them, and re-layouts  3.68 us (2%)
  other arithmetic  3.3 us (1%)
    all_to_all x1, blocking collectives, local(): lax.all_to_all(returned, SPACE, split_axis=0, concat_axis=0, tiled=True)  60.9 us
    all_to_all x1, waiting for transfers between devices, local(): lax.all_to_all(payload, SPACE, split_axis=0, concat_axis=0, tiled=True)  53.7 us
    pallas_call x1, Pallas kernels, local(): pl.pallas_call(functools.partial(project_kernel, levels=levels), out_shap...  28.4 us
    pallas_call x1, Pallas kernels, local(): pl.pallas_call(functools.partial(carry_kernel, blocks=blocks, pieces=piec...  22.7 us
    pallas_call x1, Pallas kernels, local(): pl.pallas_call(functools.partial(source_kernel, levels=levels), out_shape...  16.6 us
    pallas_call x1, Pallas kernels, local(): pl.pallas_call(functools.partial(backward_kernel, here=here, rows=rows, l...  13.3 us
    pallas_call x1, Pallas kernels, local(): pl.pallas_call(functools.partial(forward_kernel, here=here, rows=rows), o...  12.8 us
    all_to_all x1, starting transfers between devices, local(): lax.all_to_all(payload, SPACE, split_axis=0, concat_axis=0, tiled=True)  5.19 us
  transfers between devices with their start and end apart: 1, of which 1 were waited for; matrix products, arithmetic and copies ran while one was open for 1% of the time, Pallas kernels for 0%

profile of v3, /device:TPU:0, one launch (start us, length us, event | category | flops | bytes accessed | tf_op | source)
XLA Modules:
  0.0 221.3 jit_solution(193117878930493200)
XLA Ops:
  0.6 1.7 add_multiply_fusion.4.table
  2.4 16.6 %source.1 = f32[8,2,296,256]{3,2,1,0:T(8,128)} custom-call(f32[3,8,16,32,256]{4,3,2,1,0:T(8,128)} %mult.3, f32[3,8,16,32,256]{4,3,2,1,0:T(8,128)} %aux.1, f32[16,32,256]{2,1,0:T(8,128)} %start.1, f32[16,32,256]{2,1,0:T(8,128)} %end.1, f32[256,256]{1,0:T(8,128)} %add_multiply_fusion.4.table), custom_call_target="tpu_custom_call" | custom-call | tf_op jit(solution)/shard_map/source/pallas_call | solution.py:403
  18.9 5.2 %all-to-all-start = ((f32[8,2,296,256]{3,2,1,0:T(8,128)}), f32[8,2,296,256]{3,2,1,0:T(8,128)}, u32[]{:S(2)}, u32[]{:S(2)}) async-start(f32[8,2,296,256]{3,2,1,0:T(8,128)} %source.1), calls=%async_computation | async-start | bytes 9699328 | tf_op jit(solution)/shard_map/all_to_all | solution.py:418
  24.2 0.2 fusion.21.step
  24.4 0.2 fusion.29
  24.6 0.2 fusion.27
  24.8 0.3 fusion.6
  25.1 0.3 fusion.7
  25.4 0.3 fusion.13.coef
  25.7 0.0 copy-start.4
  25.7 53.7 %all-to-all-done.x = f32[8,2,296,256]{3,2,1,0:T(8,128)} async-done(((f32[8,2,296,256]{3,2,1,0:T(8,128)}), f32[8,2,296,256]{3,2,1,0:T(8,128)}, u32[]{:S(2)}, u32[]{:S(2)}) %all-to-all-start) | async-done | bytes 4849696 | tf_op jit(solution)/shard_map/all_to_all | solution.py:418
  79.4 0.0 copy-done.4
  79.4 12.8 %forward.1 = (f32[2,9,256,256]{3,2,1,0:T(8,128)}, f32[2,256,256]{2,1,0:T(8,128)}, f32[2,256,256]{2,1,0:T(8,128)}) custom-call(f32[8,2,296,256]{3,2,1,0:T(8,128)} %all-to-all-done.x, f32[256,256]{1,0:T(8,128)} %add_multiply_fusion.4.table, f32[5,256,256]{2,1,0:T(8,128)} %copy-done.4), custom_call_target="tpu_custom_call" | custom-call | tf_op jit(solution)/shard_map/forward/pallas_call | solution.py:424
  92.2 0.0 copy-start.2
  92.2 1.0 copy-done.2
  93.3 0.0 copy-start.3
  93.3 1.0 copy-done.3
  94.3 22.7 %carry.1 = (f32[2,256,256]{2,1,0:T(8,128)S(1)}, f32[2,256,256]{2,1,0:T(8,128)S(1)}) custom-call(f32[2,256,256]{2,1,0:T(8,128)S(1)} %copy-done.2, f32[2,256,256]{2,1,0:T(8,128)S(1)} %copy-done.3, f32[256,256]{1,0:T(8,128)S(1)} %fusion.21.step), custom_call_target="tpu_custom_call" | custom-call | tf_op jit(solution)/shard_map/carry/pallas_call | solution.py:442
  117.1 0.0 copy-start
  117.1 0.8 copy-done
  117.9 0.0 copy-start.1
  117.9 0.8 copy-done.1
  118.7 13.3 %backward.1 = f32[8,2,296,256]{3,2,1,0:T(8,128)} custom-call(f32[2,9,256,256]{3,2,1,0:T(8,128)} %get-tuple-element.7.modes, f32[2,256,256]{2,1,0:T(8,128)} %copy-done, f32[2,256,256]{2,1,0:T(8,128)} %copy-done.1, f32[256,256]{1,0:T(8,128)} %add_multiply_fusion.4.table, f32[5,256,256]{2,1,0:T(8,128)} %copy-done.4), custom_call_target="tpu_custom_call" | custom-call | tf_op jit(solution)/shard_map/backward/pallas_call | solution.py:455
  132.0 60.9 %all_to_all.10.x = f32[8,2,296,256]{3,2,1,0:T(8,128)} all-to-all(f32[8,2,296,256]{3,2,1,0:T(8,128)} %backward.1), channel_id=1, replica_groups=mesh['grp'=2,'px'=4,'py'=4] {'grp','px'}, dimensions={0} | all-to-all | bytes 9699328 | tf_op jit(solution)/shard_map/all_to_all | solution.py:472
  192.9 28.4 %project.1 = (f32[3,8,16,32,256]{4,3,2,1,0:T(8,128)}, f32[3,8,16,32,256]{4,3,2,1,0:T(8,128)}) custom-call(f32[8,2,296,256]{3,2,1,0:T(8,128)} %all_to_all.10.x, f32[3,8,16,32,256]{4,3,2,1,0:T(8,128)} %mult.3, f32[256,256]{1,0:T(8,128)} %add_multiply_fusion.4.table), custom_call_target="tpu_custom_call" | custom-call | tf_op jit(solution)/shard_map/project/pallas_call | solution.py:475
  (1 shorter events, 0.0 us)
Async XLA Ops:
  18.9 60.5 %all-to-all-start = ((f32[8,2,296,256]{3,2,1,0:T(8,128)}), f32[8,2,296,256]{3,2,1,0:T(8,128)}, u32[]{:S(2)}, u32[]{:S(2)}) async-start(f32[8,2,296,256]{3,2,1,0:T(8,128)} %source.1), calls=%async_computation | async-start | bytes 9699328 | tf_op jit(solution)/shard_map/all_to_all | solution.py:418
  25.7 53.7 %copy-start.4 = (f32[5,256,256]{2,1,0:T(8,128)}, f32[5,256,256]{2,1,0:T(8,128)S(1)}, u32[]{:S(2)}) copy-start(f32[5,256,256]{2,1,0:T(8,128)S(1)} %fusion.13.coef) | copy-start | bytes 3932164
  92.2 1.0 copy-start.2
  93.3 1.0 copy-start.3
  117.1 0.8 copy-start
  117.9 0.8 copy-start.1
